TPU v7x, 256 devices: a whole 4x4x8 slice. The times are simulated.
256 devices in a mesh: brick: 32 (over z, y_hi, core), chan: 8 (over y_lo, x).
Axes of the slice: x: 4, y: 4 (y_hi: 2, y_lo: 2; y = y_hi * 2 + y_lo), z: 8, core: 2. Of those that a mesh axis runs over, the one named last changes fastest.
Arguments:
- volume: bfloat16 [64, 64, 64, 256], P('brick', 'chan'), may hold values from -6 to 6
- first_weight: bfloat16 [3, 3, 3, 256, 256], replicated, may hold values from -0.078125 to 0.078125
- second_weight: bfloat16 [3, 3, 3, 256, 256], replicated, may hold values from -0.078125 to 0.078125
- coarse_weight: bfloat16 [3, 3, 3, 256, 512], P(None, None, None, None, 'chan'), may hold values from -0.078125 to 0.078125
- projection: bfloat16 [512, 256], P('chan'), may hold values from -0.25 to 0.25
Outputs:
- merged: bfloat16 [64, 64, 64, 256], P('brick', 'chan')
All inputs are finite; a program needn't handle non-finite values.
Results may differ from a plain program's by a relative error of at most 0.011.
Values may be sent and summed in bfloat16 or wider, within the bound.
A program may use at most 64 MiB of HBM per device.

v0:
```python
import jax
import jax.numpy as jnp
from jax import lax
from jax.sharding import PartitionSpec as P


def extended(block, sides, width):
    for axis, dim in sides:
        count = lax.axis_size(axis)
        forward = [(i, i + 1) for i in range(count - 1)]
        backward = [(target, source) for source, target in forward]
        low = lax.ppermute(
            lax.slice_in_dim(block, block.shape[dim] - width, None, axis=dim), axis, forward
        )
        high = lax.ppermute(lax.slice_in_dim(block, 0, width, axis=dim), axis, backward)
        block = jnp.concatenate([low, block, high], axis=dim)
    return block


def joined_along(pieces, dim):
    pieces = jnp.moveaxis(pieces, 0, dim)
    shape = pieces.shape
    return pieces.reshape(*shape[:dim], shape[dim] * shape[dim + 1], *shape[dim + 2 :])


def copy_for_each(shard, axis):
    copies = jnp.broadcast_to(shard, (lax.axis_size(axis), *shard.shape))
    return lax.all_to_all(copies, axis, split_axis=0, concat_axis=0, tiled=True)


def gathered_copies(shard, axis, dim):
    return joined_along(copy_for_each(shard, axis), dim)


def split_up(shard, dim, size):
    before, after = (shard.shape[:dim], shard.shape[dim + 1 :])
    return jnp.moveaxis(shard.reshape(*before, size, -1, *after), dim, 0)


def sent_and_summed(shard, axis, dim):
    pieces = split_up(shard, dim, lax.axis_size(axis))
    arrived = lax.all_to_all(pieces, axis, split_axis=0, concat_axis=0, tiled=True)
    return arrived.astype(jnp.float32).sum(axis=0)


def convolve(padded, weight):
    rows_x = padded.shape[0] - 2
    rows_y = padded.shape[1] - 2
    rows_z = padded.shape[2] - 2
    inputs_count = padded.shape[3]
    outputs_count = weight.shape[4]
    total = jnp.zeros((rows_x * rows_y * rows_z, outputs_count), jnp.float32)
    for offset_x in range(3):
        for offset_y in range(3):
            for offset_z in range(3):
                window = padded[
                    offset_x : offset_x + rows_x,
                    offset_y : offset_y + rows_y,
                    offset_z : offset_z + rows_z,
                ]
                window = window.reshape(-1, inputs_count)
                total = total + jnp.dot(
                    window, weight[offset_x, offset_y, offset_z], preferred_element_type=jnp.float32
                )
    return total.reshape(rows_x, rows_y, rows_z, outputs_count)


def fine_layer(field, weight):
    padded = extended(field, (("brick", 0), ("chan", 1)), 1)
    padded = jnp.pad(padded, ((0, 0), (0, 0), (1, 1), (0, 0)))
    return jnp.maximum(convolve(padded, weight), 0.0).astype(jnp.bfloat16)


def shards(volume, first_weight, second_weight, coarse_weight, projection):
    layer_one = fine_layer(volume, first_weight)
    skipped = fine_layer(layer_one, second_weight)
    size_x, size_y, size_z, channels_in = skipped.shape
    blocks = skipped.astype(jnp.float32).reshape(
        size_x // 2, 2, size_y // 2, 2, size_z // 2, 2, channels_in
    )
    pooled = jnp.mean(blocks, axis=(1, 3, 5)).astype(jnp.bfloat16)
    brick_cells = gathered_copies(pooled, "chan", 1)
    padded = extended(brick_cells, (("brick", 0),), 1)
    padded = jnp.pad(padded, ((0, 0), (1, 1), (1, 1), (0, 0)))
    coarse = jnp.maximum(convolve(padded, coarse_weight), 0.0).astype(jnp.bfloat16)
    coarse_shape = coarse.shape
    terms = jnp.dot(
        coarse.reshape(-1, coarse_shape[3]), projection, preferred_element_type=jnp.float32
    )
    terms = terms.reshape(coarse_shape[0], coarse_shape[1], coarse_shape[2], channels_in)
    lifted = sent_and_summed(terms.astype(jnp.bfloat16), "chan", 1)
    upsampled = jnp.repeat(jnp.repeat(jnp.repeat(lifted, 2, axis=0), 2, axis=1), 2, axis=2)
    return (skipped.astype(jnp.float32) + upsampled).astype(jnp.bfloat16)


def solution(mesh):
    in_specs = (
        P("brick", "chan", None, None),
        P(),
        P(),
        P(None, None, None, None, "chan"),
        P("chan", None),
    )
    out_specs = P("brick", "chan", None, None)
    return jax.shard_map(shards, mesh=mesh, in_specs=in_specs, out_specs=out_specs, check_vma=False)
```

profile of v0, /device:TPU:112, one launch (start us, length us, event | category | flops | bytes accessed | tf_op | source)
XLA Modules:
  0.0 138.2 jit_solution(7951131302254155916)
XLA Ops:
  0.0 1.2 fusion.320
  1.2 2.1 %collective-permute-start.1 = (bf16[1,8,64,256]{3,2,1,0:T(8,128)(2,1)S(1)}, bf16[1,8,64,256]{3,2,1,0:T(8,128)(2,1)S(1)}, u32[]{:S(2)}, u32[]{:S(2)}) collective-permute-start(bf16[1,8,64,256]{3,2,1,0:T(8,128)(2,1)S(1)} %get-tuple-element.93), channel_id=1, source_target_pairs={{8,0},{16,8},{24,16},{32,24},{40,32},{48,40},{56,48},{64,56},{72,6... | collective-permute-start | bytes 786440 | tf_op jit(solution)/shard_map/ppermute | solution.py:15
  3.3 2.4 %collective-permute-start = (bf16[1,8,64,256]{3,2,1,0:T(8,128)(2,1)S(1)}, bf16[1,8,64,256]{3,2,1,0:T(8,128)(2,1)S(1)}, u32[]{:S(2)}, u32[]{:S(2)}) collective-permute-start(bf16[1,8,64,256]{3,2,1,0:T(8,128)(2,1)S(1)} %get-tuple-element.94), channel_id=1, source_target_pairs={{0,8},{8,16},{16,24},{24,32},{32,40},{40,48},{48,56},{56,64},{64,7... | collective-permute-start | bytes 786440 | tf_op jit(solution)/shard_map/ppermute | solution.py:12
  5.7 1.4 fusion.150
  7.1 8.2 %collective-permute-done = bf16[1,8,64,256]{3,2,1,0:T(8,128)(2,1)S(1)} collective-permute-done((bf16[1,8,64,256]{3,2,1,0:T(8,128)(2,1)S(1)}, bf16[1,8,64,256]{3,2,1,0:T(8,128)(2,1)S(1)}, u32[]{:S(2)}, u32[]{:S(2)}) %collective-permute-start) | collective-permute-done | bytes 262176 | tf_op jit(solution)/shard_map/ppermute | solution.py:12
  15.8 3.4 %collective-permute-start.2 = (bf16[4,1,64,256]{3,2,1,0:T(8,128)(2,1)S(1)}, bf16[4,1,64,256]{3,2,1,0:T(8,128)(2,1)S(1)}, u32[]{:S(2)}, u32[]{:S(2)}) collective-permute-start(bf16[4,1,64,256]{3,2,1,0:T(8,128)(2,1)S(1)} %get-tuple-element.84), channel_id=1, source_target_pairs={{0,1},{1,2},{2,3},{3,4},{4,5},{5,6},{6,7},{8,9},{9,10},{10,11},{11... | collective-permute-start | bytes 393224 | tf_op jit(solution)/shard_map/ppermute | solution.py:12
  19.3 1.3 collective-permute-start.3
  20.8 0.9 collective-permute-done.2
  21.7 4.4 %collective-permute-done.3 = bf16[4,1,64,256]{3,2,1,0:T(8,128)(2,1)S(1)} collective-permute-done((bf16[4,1,64,256]{3,2,1,0:T(8,128)(2,1)S(1)}, bf16[4,1,64,256]{3,2,1,0:T(8,128)(2,1)S(1)}, u32[]{:S(2)}, u32[]{:S(2)}) %collective-permute-start.3) | collective-permute-done | bytes 131104 | tf_op jit(solution)/shard_map/ppermute | solution.py:15
  26.6 0.3 fusion.174
  26.9 0.3 fusion.156
  27.2 0.3 fusion.127
  27.8 0.3 fusion.162
  28.1 0.8 fusion.14
  28.9 3.1 %fusion.315 = (bf16[2,8,64,256]{3,2,1,0:T(8,128)(2,1)S(1)}, bf16[2,8,64,256]{3,2,1,0:T(8,128)(2,1)S(1)}, bf16[2,8,64,256]{3,2,1,0:T(8,128)(2,1)S(1)}, bf16[2,8,6...) fusion(bf16[4,10,66,256]{3,2,1,0:T(8,128)(2,1)S(1)} %fusion.14), kind=kLoop, calls=%fused_computation.360 | loop fusion | bytes 18874368 | tf_op jit(solution)/shard_map/slice | solution.py:56
  32.4 0.3 fusion.176
  32.7 0.3 fusion.131
  33.3 0.3 fusion.137
  33.9 0.3 fusion.143
  34.2 0.3 fusion.147
  34.5 0.3 fusion.152
  34.8 0.3 fusion.154
  35.4 0.3 fusion.160
  35.7 0.3 fusion.164
  36.0 0.3 fusion.166
  36.3 0.3 fusion.170
  36.6 0.3 fusion.172
  36.9 1.3 fusion.125
  38.2 2.6 %fusion.46 = bf16[1024,256]{1,0:T(8,128)(2,1)S(1)} fusion(f32[1024,256]{1,0:T(8,128)} %fusion.125, f32[1024,256]{1,0:T(8,128)S(1)} %fusion.127, f32[1024,256]{1,0:T(8,128)S(1)} %fusion.129, f32[1024,256]{1,0:T(8,128)S(1)} %fusion.131, f32[1024,256]{1,0:T(8,128)S(1)} %fusion.133, f32[1024,256]{1,0:T(8,128)S(1)} %fusion.135, f32[1024,256]{1,0:T(8,128)S(1)} %fusion.137, ...), kind=kOutput, calls=%fused_computation.67 | convolution fusion | flops 141557760 | bytes 28442624 | tf_op jit(solution)/shard_map/dot_general | solution.py:62
  40.9 2.2 %collective-permute-start.5 = (bf16[1,8,64,256]{3,2,1,0:T(8,128)(2,1)S(1)}, bf16[1,8,64,256]{3,2,1,0:T(8,128)(2,1)S(1)}, u32[]{:S(2)}, u32[]{:S(2)}) collective-permute-start(bf16[1,8,64,256]{3,2,1,0:T(8,128)(2,1)S(1)} %bitcast.510), channel_id=1, source_target_pairs={{8,0},{16,8},{24,16},{32,24},{40,32},{48,40},{56,48},{64,56},{72,6... | collective-permute-start | bytes 786440 | tf_op jit(solution)/shard_map/ppermute | solution.py:15
  43.1 2.4 %collective-permute-start.4 = (bf16[1,8,64,256]{3,2,1,0:T(8,128)(2,1)S(1)}, bf16[1,8,64,256]{3,2,1,0:T(8,128)(2,1)S(1)}, u32[]{:S(2)}, u32[]{:S(2)}) collective-permute-start(bf16[1,8,64,256]{3,2,1,0:T(8,128)(2,1)S(1)} %bitcast.509), channel_id=1, source_target_pairs={{0,8},{8,16},{16,24},{24,32},{32,40},{40,48},{48,56},{56,64},{64,7... | collective-permute-start | bytes 786440 | tf_op jit(solution)/shard_map/ppermute | solution.py:12
  45.5 1.2 fusion.99
  46.9 7.6 %collective-permute-done.4 = bf16[1,8,64,256]{3,2,1,0:T(8,128)(2,1)S(1)} collective-permute-done((bf16[1,8,64,256]{3,2,1,0:T(8,128)(2,1)S(1)}, bf16[1,8,64,256]{3,2,1,0:T(8,128)(2,1)S(1)}, u32[]{:S(2)}, u32[]{:S(2)}) %collective-permute-start.4) | collective-permute-done | bytes 262176 | tf_op jit(solution)/shard_map/ppermute | solution.py:12
  54.6 3.4 %collective-permute-start.6 = (bf16[4,1,64,256]{3,2,1,0:T(8,128)(2,1)S(1)}, bf16[4,1,64,256]{3,2,1,0:T(8,128)(2,1)S(1)}, u32[]{:S(2)}, u32[]{:S(2)}) collective-permute-start(bf16[4,1,64,256]{3,2,1,0:T(8,128)(2,1)S(1)} %get-tuple-element.79), channel_id=1, source_target_pairs={{0,1},{1,2},{2,3},{3,4},{4,5},{5,6},{6,7},{8,9},{9,10},{10,11},{11... | collective-permute-start | bytes 393224 | tf_op jit(solution)/shard_map/ppermute | solution.py:12
  58.0 1.5 %collective-permute-start.7 = (bf16[4,1,64,256]{3,2,1,0:T(8,128)(2,1)S(1)}, bf16[4,1,64,256]{3,2,1,0:T(8,128)(2,1)S(1)}, u32[]{:S(2)}, u32[]{:S(2)}) collective-permute-start(bf16[4,1,64,256]{3,2,1,0:T(8,128)(2,1)S(1)} %get-tuple-element.80), channel_id=1, source_target_pairs={{1,0},{2,1},{3,2},{4,3},{5,4},{6,5},{7,6},{9,8},{10,9},{11,10},{12... | collective-permute-start | bytes 393224 | tf_op jit(solution)/shard_map/ppermute | solution.py:15
  59.6 0.3 fusion.84
  59.9 0.3 fusion.115
  60.5 4.4 %collective-permute-done.7 = bf16[4,1,64,256]{3,2,1,0:T(8,128)(2,1)S(1)} collective-permute-done((bf16[4,1,64,256]{3,2,1,0:T(8,128)(2,1)S(1)}, bf16[4,1,64,256]{3,2,1,0:T(8,128)(2,1)S(1)}, u32[]{:S(2)}, u32[]{:S(2)}) %collective-permute-start.7) | collective-permute-done | bytes 131104 | tf_op jit(solution)/shard_map/ppermute | solution.py:15
  65.3 0.3 fusion.89
  66.5 0.3 fusion.78
  66.9 0.3 fusion.109
  67.2 0.8 select_maximum_fusion.2
  68.0 3.3 %fusion.314 = (bf16[2,8,64,256]{3,2,1,0:T(8,128)(2,1)S(1)}, bf16[2,8,64,256]{3,2,1,0:T(8,128)(2,1)S(1)}, bf16[2,8,64,256]{3,2,1,0:T(8,128)(2,1)S(1)}, bf16[2,8,6...) fusion(bf16[4,10,66,256]{3,2,1,0:T(8,128)(2,1)S(1)} %select_max, ...), kind=kLoop, calls=%fused_computation.359 | loop fusion | bytes 18874368 | tf_op jit(solution)/shard_map/slice | solution.py:56
  74.9 0.6 fusion.30
  75.5 0.4 fusion.28
  75.9 0.4 fusion.26
  76.3 0.4 fusion.24
  76.7 0.6 fusion.22
  77.3 0.3 fusion.45
  77.6 0.6 reshape.384
  78.2 0.5 reduce_sum.18
  78.8 14.5 %all_to_all.10 = bf16[8,1,4,32,256]{4,3,2,1,0:T(8,128)(2,1)S(1)} all-to-all(bf16[8,1,4,32,256]{4,3,2,1,0:T(8,128)(2,1)S(1)} %broadcast_in_dim.16), channel_id=1, replica_groups=mesh['brick'=32,'chan'=8] {'chan'}, dimensions={0} | all-to-all | bytes 1048576 | tf_op jit(solution)/shard_map/all_to_all | solution.py:28
  93.4 1.9 %collective-permute-start.9 = (bf16[1,32,32,256]{3,2,1,0:T(8,128)(2,1)S(1)}, bf16[1,32,32,256]{3,2,1,0:T(8,128)(2,1)S(1)}, u32[]{:S(2)}, u32[]{:S(2)}) collective-permute-start(bf16[1,32,32,256]{3,2,1,0:T(8,128)(2,1)S(1)} %bitcast.424), channel_id=1, source_target_pairs={{8,0},{16,8},{24,16},{32,24},{40,32},{48,40},{56,48},{64,56},{72,6... | collective-permute-start | bytes 1572872 | tf_op jit(solution)/shard_map/ppermute | solution.py:15
  95.3 2.6 %collective-permute-start.8 = (bf16[1,32,32,256]{3,2,1,0:T(8,128)(2,1)S(1)}, bf16[1,32,32,256]{3,2,1,0:T(8,128)(2,1)S(1)}, u32[]{:S(2)}, u32[]{:S(2)}) collective-permute-start(bf16[1,32,32,256]{3,2,1,0:T(8,128)(2,1)S(1)} %bitcast.425), channel_id=1, source_target_pairs={{0,8},{8,16},{16,24},{24,32},{32,40},{40,48},{48,56},{56,64},{64,7... | collective-permute-start | bytes 1572872 | tf_op jit(solution)/shard_map/ppermute | solution.py:12
  98.2 9.4 %collective-permute-done.9 = bf16[1,32,32,256]{3,2,1,0:T(8,128)(2,1)S(1)} collective-permute-done((bf16[1,32,32,256]{3,2,1,0:T(8,128)(2,1)S(1)}, bf16[1,32,32,256]{3,2,1,0:T(8,128)(2,1)S(1)}, u32[]{:S(2)}, u32[]{:S(2)}) %collective-permute-start.9) | collective-permute-done | bytes 524320 | tf_op jit(solution)/shard_map/ppermute | solution.py:15
  107.6 4.5 %collective-permute-done.8 = bf16[1,32,32,256]{3,2,1,0:T(8,128)(2,1)S(1)} collective-permute-done((bf16[1,32,32,256]{3,2,1,0:T(8,128)(2,1)S(1)}, bf16[1,32,32,256]{3,2,1,0:T(8,128)(2,1)S(1)}, u32[]{:S(2)}, u32[]{:S(2)}) %collective-permute-start.8) | collective-permute-done | bytes 524320 | tf_op jit(solution)/shard_map/ppermute | solution.py:12
  112.0 1.0 select_maximum_fusion
  113.1 0.7 fusion.313
  113.7 3.0 %fusion.312 = (bf16[1,32,32,256]{3,2,1,0:T(8,128)(2,1)S(1)}, bf16[1,32,32,256]{3,2,1,0:T(8,128)(2,1)S(1)}, bf16[1,32,32,256]{3,2,1,0:T(8,128)(2,1)S(1)}, bf16[1,...) fusion(bf16[3,34,34,256]{3,2,1,0:T(8,128)(2,1)S(1)} %select_max, ...), kind=kLoop, calls=%fused_computation.357 | loop fusion | bytes 19922944 | tf_op jit(solution)/shard_map/slice | solution.py:56
  123.6 0.3 fusion.59
  123.9 0.3 fusion.72
  124.7 11.8 %all_to_all.11 = bf16[8,1,4,32,256]{4,3,2,1,0:T(8,128)(2,1)S(1)} all-to-all(bf16[8,1,4,32,256]{4,3,2,1,0:T(8,128)(2,1)S(1)} %bitcast.501), channel_id=1, replica_groups=mesh['brick'=32,'chan'=8] {'chan'}, dimensions={0} | all-to-all | bytes 1048576 | tf_op jit(solution)/shard_map/all_to_all | solution.py:42
  136.9 0.4 broadcast_in_dim.20
  137.2 0.9 add_convert_fusion
  (78 shorter events, 16.3 us)
Async XLA Ops:
  0.0 124.5 %copy-start = (bf16[64,256]{1,0:T(8,128)(2,1)S(1)}, bf16[64,256]{1,0:T(8,128)(2,1)}, u32[]{:S(2)}) copy-start(bf16[64,256]{1,0:T(8,128)(2,1)} %param.9) | copy-start | bytes 98308
  0.0 15.3 %copy-start.1 = (bf16[2,8,64,256]{3,2,1,0:T(8,128)(2,1)S(1)}, bf16[2,8,64,256]{3,2,1,0:T(8,128)(2,1)}, u32[]{:S(2)}) copy-start(bf16[2,8,64,256]{3,2,1,0:T(8,128)(2,1)} %param.5) | copy-start | bytes 1572868
  0.0 15.5 %copy-start.3 = (bf16[3,3,3,256,256]{4,3,2,1,0:T(8,128)(2,1)S(1)}, bf16[3,3,3,256,256]{4,3,2,1,0:T(8,128)(2,1)}, u32[]{:S(2)}) copy-start(bf16[3,3,3,256,256]{4,3,2,1,0:T(8,128)(2,1)} %param.6) | copy-start | bytes 10616836
  1.2 14.1 %collective-permute-start.1 = (bf16[1,8,64,256]{3,2,1,0:T(8,128)(2,1)S(1)}, bf16[1,8,64,256]{3,2,1,0:T(8,128)(2,1)S(1)}, u32[]{:S(2)}, u32[]{:S(2)}) collective-permute-start(bf16[1,8,64,256]{3,2,1,0:T(8,128)(2,1)S(1)} %get-tuple-element.93), channel_id=1, source_target_pairs={{8,0},{16,8},{24,16},{32,24},{40,32},{48,40},{56,48},{64,56},{72,6... | collective-permute-start | bytes 786440 | tf_op jit(solution)/shard_map/ppermute | solution.py:15
  3.3 12.0 %collective-permute-start = (bf16[1,8,64,256]{3,2,1,0:T(8,128)(2,1)S(1)}, bf16[1,8,64,256]{3,2,1,0:T(8,128)(2,1)S(1)}, u32[]{:S(2)}, u32[]{:S(2)}) collective-permute-start(bf16[1,8,64,256]{3,2,1,0:T(8,128)(2,1)S(1)} %get-tuple-element.94), channel_id=1, source_target_pairs={{0,8},{8,16},{16,24},{24,32},{32,40},{40,48},{48,56},{56,64},{64,7... | collective-permute-start | bytes 786440 | tf_op jit(solution)/shard_map/ppermute | solution.py:12
  15.8 5.9 %collective-permute-start.2 = (bf16[4,1,64,256]{3,2,1,0:T(8,128)(2,1)S(1)}, bf16[4,1,64,256]{3,2,1,0:T(8,128)(2,1)S(1)}, u32[]{:S(2)}, u32[]{:S(2)}) collective-permute-start(bf16[4,1,64,256]{3,2,1,0:T(8,128)(2,1)S(1)} %get-tuple-element.84), channel_id=1, source_target_pairs={{0,1},{1,2},{2,3},{3,4},{4,5},{5,6},{6,7},{8,9},{9,10},{10,11},{11... | collective-permute-start | bytes 393224 | tf_op jit(solution)/shard_map/ppermute | solution.py:12
  19.3 6.9 %collective-permute-start.3 = (bf16[4,1,64,256]{3,2,1,0:T(8,128)(2,1)S(1)}, bf16[4,1,64,256]{3,2,1,0:T(8,128)(2,1)S(1)}, u32[]{:S(2)}, u32[]{:S(2)}) collective-permute-start(bf16[4,1,64,256]{3,2,1,0:T(8,128)(2,1)S(1)} %get-tuple-element.85), channel_id=1, source_target_pairs={{1,0},{2,1},{3,2},{4,3},{5,4},{6,5},{7,6},{9,8},{10,9},{11,10},{12... | collective-permute-start | bytes 393224 | tf_op jit(solution)/shard_map/ppermute | solution.py:15
  40.8 18.8 %copy-start.2 = (bf16[3,3,3,256,256]{4,3,2,1,0:T(8,128)(2,1)S(1)}, bf16[3,3,3,256,256]{4,3,2,1,0:T(8,128)(2,1)}, u32[]{:S(2)}) copy-start(bf16[3,3,3,256,256]{4,3,2,1,0:T(8,128)(2,1)} %param.7) | copy-start | bytes 10616836
  40.9 6.1 %collective-permute-start.5 = (bf16[1,8,64,256]{3,2,1,0:T(8,128)(2,1)S(1)}, bf16[1,8,64,256]{3,2,1,0:T(8,128)(2,1)S(1)}, u32[]{:S(2)}, u32[]{:S(2)}) collective-permute-start(bf16[1,8,64,256]{3,2,1,0:T(8,128)(2,1)S(1)} %bitcast.510), channel_id=1, source_target_pairs={{8,0},{16,8},{24,16},{32,24},{40,32},{48,40},{56,48},{64,56},{72,6... | collective-permute-start | bytes 786440 | tf_op jit(solution)/shard_map/ppermute | solution.py:15
  43.1 11.5 %collective-permute-start.4 = (bf16[1,8,64,256]{3,2,1,0:T(8,128)(2,1)S(1)}, bf16[1,8,64,256]{3,2,1,0:T(8,128)(2,1)S(1)}, u32[]{:S(2)}, u32[]{:S(2)}) collective-permute-start(bf16[1,8,64,256]{3,2,1,0:T(8,128)(2,1)S(1)} %bitcast.509), channel_id=1, source_target_pairs={{0,8},{8,16},{16,24},{24,32},{32,40},{40,48},{48,56},{56,64},{64,7... | collective-permute-start | bytes 786440 | tf_op jit(solution)/shard_map/ppermute | solution.py:12
  54.6 5.9 %collective-permute-start.6 = (bf16[4,1,64,256]{3,2,1,0:T(8,128)(2,1)S(1)}, bf16[4,1,64,256]{3,2,1,0:T(8,128)(2,1)S(1)}, u32[]{:S(2)}, u32[]{:S(2)}) collective-permute-start(bf16[4,1,64,256]{3,2,1,0:T(8,128)(2,1)S(1)} %get-tuple-element.79), channel_id=1, source_target_pairs={{0,1},{1,2},{2,3},{3,4},{4,5},{5,6},{6,7},{8,9},{9,10},{10,11},{11... | collective-permute-start | bytes 393224 | tf_op jit(solution)/shard_map/ppermute | solution.py:12
  58.0 6.9 %collective-permute-start.7 = (bf16[4,1,64,256]{3,2,1,0:T(8,128)(2,1)S(1)}, bf16[4,1,64,256]{3,2,1,0:T(8,128)(2,1)S(1)}, u32[]{:S(2)}, u32[]{:S(2)}) collective-permute-start(bf16[4,1,64,256]{3,2,1,0:T(8,128)(2,1)S(1)} %get-tuple-element.80), channel_id=1, source_target_pairs={{1,0},{2,1},{3,2},{4,3},{5,4},{6,5},{7,6},{9,8},{10,9},{11,10},{12... | collective-permute-start | bytes 393224 | tf_op jit(solution)/shard_map/ppermute | solution.py:15
  77.3 20.6 %copy-start.4 = (bf16[3,3,3,256,64]{3,4,2,1,0:T(8,128)(2,1)S(1)}, bf16[3,3,3,256,64]{3,4,2,1,0:T(8,128)(2,1)}, u32[]{:S(2)}) copy-start(bf16[3,3,3,256,64]{3,4,2,1,0:T(8,128)(2,1)} %param.8) | copy-start | bytes 2654212
  93.4 14.2 %collective-permute-start.9 = (bf16[1,32,32,256]{3,2,1,0:T(8,128)(2,1)S(1)}, bf16[1,32,32,256]{3,2,1,0:T(8,128)(2,1)S(1)}, u32[]{:S(2)}, u32[]{:S(2)}) collective-permute-start(bf16[1,32,32,256]{3,2,1,0:T(8,128)(2,1)S(1)} %bitcast.424), channel_id=1, source_target_pairs={{8,0},{16,8},{24,16},{32,24},{40,32},{48,40},{56,48},{64,56},{72,6... | collective-permute-start | bytes 1572872 | tf_op jit(solution)/shard_map/ppermute | solution.py:15
  95.3 16.7 %collective-permute-start.8 = (bf16[1,32,32,256]{3,2,1,0:T(8,128)(2,1)S(1)}, bf16[1,32,32,256]{3,2,1,0:T(8,128)(2,1)S(1)}, u32[]{:S(2)}, u32[]{:S(2)}) collective-permute-start(bf16[1,32,32,256]{3,2,1,0:T(8,128)(2,1)S(1)} %bitcast.425), channel_id=1, source_target_pairs={{0,8},{8,16},{16,24},{24,32},{32,40},{40,48},{48,56},{56,64},{64,7... | collective-permute-start | bytes 1572872 | tf_op jit(solution)/shard_map/ppermute | solution.py:12
where the time goes:
time: 139 us; the launch traced here: 138 us
  waiting for transfers between devices  39.9 us (29%)
  matrix products  30.3 us (22%)
  blocking collectives  26.3 us (19%)
  starting transfers between devices  23.1 us (17%)
  local copies, waits for them, and re-layouts  13.1 us (9%)
  other arithmetic  4.88 us (4%)
    dot_general x81, matrix products, convolve(): jnp.dot(window, weight[offset_x, offset_y, offset_z], preferred_element_t...  30.1 us
    ppermute x5, waiting for transfers between devices, extended(): lax.ppermute(lax.slice_in_dim(block, block.shape[dim] - width, None, axis...  21.5 us
    ppermute x5, waiting for transfers between devices, extended(): lax.ppermute(lax.slice_in_dim(block, 0, width, axis=dim), axis, backward)  18.4 us
    all_to_all x1, blocking collectives, copy_for_each(): return lax.all_to_all(copies, axis, split_axis=0, concat_axis=0, tiled=True)  14.5 us
    ppermute x5, starting transfers between devices, extended(): lax.ppermute(lax.slice_in_dim(block, block.shape[dim] - width, None, axis...  14.2 us
    all_to_all x1, blocking collectives, sent_and_summed(): lax.all_to_all(pieces, axis, split_axis=0, concat_axis=0, tiled=True)  11.8 us
    slice x5, local copies, waits for them, and re-layouts, convolve(): padded[offset_x:offset_x + rows_x, offset_y:offset_y + rows_y, offset_z:o...  10.3 us
    ppermute x5, starting transfers between devices, extended(): lax.ppermute(lax.slice_in_dim(block, 0, width, axis=dim), axis, backward)  8.91 us
  transfers between devices with their start and end apart: 10, of which 9 were waited for; matrix products, arithmetic and copies ran while one was open for 3% of the time, Pallas kernels for 0%

commit v1 on v0

v1 whole, which is shorter than its diff:
```python
import functools

import jax
import jax.numpy as jnp
from jax import lax
from jax.experimental import pallas as pl
from jax.experimental.pallas import tpu as pltpu
from jax.sharding import PartitionSpec as P

MESH = pl.DeviceIdType.MESH
F32 = jnp.float32
BF16 = jnp.bfloat16


def level(
    nb, nc, vol, w1h, w2h, wch, prh, out,
    x, y, w1, w2, wc, wcr, pg, xc, con, rec, prj, prr, acc1, acc2, skip, tmp,
    loc, s1, r1, s2, r2, sp, rp, sg, rg, sc, rc,
):
    b = lax.axis_index("brick")
    c = lax.axis_index("chan")
    q = lax.rem(b, 2)
    slow = lax.rem(b + 2 * q - 1 + nb, nb)
    fast = lax.rem(b + 1 - 2 * q + nb, nb)
    below = lax.rem(b - 1 + nb, nb)
    above = lax.rem(b + 1, nb)

    def chan(d):
        return lax.rem(c + d, nc)

    loads = [
        pltpu.make_async_copy(vol.at[q], x.at[1, 1, pl.ds(1, 8)], loc.at[0]),
        pltpu.make_async_copy(vol.at[1 - q], x.at[1, 2, pl.ds(1, 8)], loc.at[1]),
        pltpu.make_async_copy(w1h, w1, loc.at[2]),
        pltpu.make_async_copy(prh, prj.at[c], loc.at[3]),
        pltpu.make_async_copy(wch, wc, loc.at[4]),
        pltpu.make_async_copy(w2h, w2, loc.at[5]),
    ]
    for load in loads:
        load.start()

    barrier = pltpu.get_barrier_semaphore()
    for brick in (b, below, above):
        for d in range(nc):
            if brick is b and d == 0:
                continue
            pl.semaphore_signal(barrier, inc=1, device_id=(brick, chan(d)), device_id_type=MESH)
    loads[0].wait()
    loads[1].wait()
    pl.semaphore_wait(barrier, 3 * nc - 1)

    right, left = chan(1), chan(nc - 1)

    def halo(buf, ss, rs, u):
        far, dest = (slow, 0) if u == 0 else (fast, 3)
        p = u + 1
        plans = [
            (p, 8, 1, p, 0, (b, right)),
            (p, 1, 1, p, 9, (b, left)),
            (p, 8, 1, dest, 0, (far, right)),
            (p, 1, 1, dest, 9, (far, left)),
            (p, 1, 8, dest, 1, (far, c)),
        ]
        return [
            pltpu.make_async_remote_copy(
                buf.at[1, src, pl.ds(row, n)], buf.at[1, dst, pl.ds(to, n)],
                ss.at[u, i], rs.at[u, i], device_id=who, device_id_type=MESH,
            )
            for i, (src, row, n, dst, to, who) in enumerate(plans)
        ]

    first = [halo(x, s1, r1, 0), halo(x, s1, r1, 1)]
    for copies in first:
        for copy in copies:
            copy.start()

    loads[3].wait()
    gifts = [
        pltpu.make_async_remote_copy(
            prj.at[c], prj.at[c], sp.at[d], rp.at[d], device_id=(b, chan(d)), device_id_type=MESH
        )
        for d in range(1, nc)
    ]
    for gift in gifts:
        gift.start()

    zero_row = jnp.zeros((1, 256), BF16)

    def spread(buf, p, row, v):
        buf[0, p, row] = jnp.concatenate([zero_row, v[:-1]], axis=0)
        buf[2, p, row] = jnp.concatenate([v[1:], zero_row], axis=0)

    def spread_rows(buf, p, start, n):
        def body(i, _):
            spread(buf, p, start + i, buf[1, p, start + i])
            return 0
        lax.fori_loop(0, n, body, 0)

    has_low, has_high = c > 0, c < nc - 1
    has_slow = jnp.logical_and(slow != b + nb - 1, slow != b + 1 - nb)

    def masked(buf, p, row, valid):
        v = jnp.where(valid, buf[1, p, row].astype(F32), 0.0).astype(BF16)
        buf[1, p, row] = v
        spread(buf, p, row, v)

    def edge_rows(buf, copies, u):
        copies[u][0].wait_recv()
        copies[u][1].wait_recv()
        masked(buf, u + 1, 0, has_low)
        masked(buf, u + 1, 9, has_high)

    def plane_halo(buf, copies, u):
        p = 0 if u == 0 else 3
        for k in (2, 3, 4):
            copies[u][k].wait_recv()
        if u == 0:
            masked(buf, p, 0, jnp.logical_and(has_low, has_slow))
            masked(buf, p, 9, jnp.logical_and(has_high, has_slow))

            def body(i, _):
                masked(buf, p, 1 + i, has_slow)
                return 0
            lax.fori_loop(0, 8, body, 0)
        else:
            masked(buf, p, 0, has_low)
            masked(buf, p, 9, has_high)
            spread_rows(buf, p, 1, 8)

    def taps(buf, w, u, i):
        lhs = jnp.concatenate(
            [buf[k, u + i, j : j + 8].reshape(512, 256) for j in range(3) for k in range(3)], axis=1
        )
        return jnp.dot(lhs, w[i + q * (2 - 2 * i)], preferred_element_type=F32)

    def finish_one(u):
        def body(r, _):
            v = jnp.maximum(acc1[u, pl.ds(pl.multiple_of(r * 64, 64), 64)], 0.0).astype(BF16)
            y[1, u + 1, 1 + r] = v
            spread(y, u + 1, 1 + r, v)
            return 0
        lax.fori_loop(0, 8, body, 0)

    spread_rows(x, 1, 1, 8)
    spread_rows(x, 2, 1, 8)
    loads[2].wait()
    edge_rows(x, first, 1)
    edge_rows(x, first, 0)
    acc1[1] = taps(x, w1, 1, 0) + taps(x, w1, 1, 1)
    acc1[0] = taps(x, w1, 0, 1) + taps(x, w1, 0, 2)
    plane_halo(x, first, 1)
    acc1[1] += taps(x, w1, 1, 2)
    finish_one(1)
    second = [halo(y, s2, r2, 0), halo(y, s2, r2, 1)]
    for copy in second[1]:
        copy.start()
    plane_halo(x, first, 0)
    acc1[0] += taps(x, w1, 0, 0)
    finish_one(0)
    for copy in second[0]:
        copy.start()

    loads[5].wait()
    edge_rows(y, second, 1)
    acc2[1] = taps(y, w2, 1, 1)
    acc2[0] = taps(y, w2, 0, 2)
    plane_halo(y, second, 1)
    acc2[1] += taps(y, w2, 1, 2)
    edge_rows(y, second, 0)
    acc2[1] += taps(y, w2, 1, 0)
    acc2[0] += taps(y, w2, 0, 1)

    loads[4].wait()
    none = jnp.zeros((256, 64), BF16)

    def weight_block(jk, _):
        wcr[pl.ds(pl.multiple_of(jk * 256, 256), 256)] = jnp.concatenate(
            [wc[jk], wc[9 + jk], wc[18 + jk], none], axis=1
        )
        return 0
    lax.fori_loop(0, 9, weight_block, 0)
    for gift in gifts:
        gift.wait()
    prr[...] = jnp.zeros_like(prr)
    for k in range(nc):
        prr[pl.ds(k * 128, 64), 0:256] = prj[k]
        prr[pl.ds(k * 128 + 64, 64), 256:512] = prj[k]

    plane_halo(y, second, 0)
    acc2[0] += taps(y, w2, 0, 0)

    def pool(r, _):
        total = jnp.zeros((64, 256), F32)
        for u in range(2):
            for s in range(2):
                rows = pl.ds(pl.multiple_of(r * 128 + s * 64, 64), 64)
                v = jnp.maximum(acc2[u, rows], 0.0).astype(BF16)
                skip[u, 2 * r + s] = v
                total = total + v.astype(F32)
        halves = []
        for h in range(2):
            tmp[r, h] = total[:, h * 128 : h * 128 + 128]
            even = tmp[r, h, pl.ds(0, 32, stride=2)]
            odd = tmp[r, h, pl.ds(1, 32, stride=2)]
            halves.append(((even + odd) * 0.125).astype(BF16))
        pg[c, r] = jnp.concatenate(halves, axis=1)
        return 0
    lax.fori_loop(0, 4, pool, 0)

    shares = [
        pltpu.make_async_remote_copy(
            pg.at[c], pg.at[c], sg.at[d], rg.at[d], device_id=(b, chan(d)), device_id_type=MESH
        )
        for d in range(1, nc)
    ]
    for share in shares:
        share.start()

    blank = jnp.zeros((32, 256), BF16)
    for k in range(3):
        xc[k, 0] = blank
        xc[k, 4 * nc + 1] = blank

    def place(block):
        def body(r, _):
            v = pg[block, r]
            row = 1 + block * 4 + r
            xc[1, row] = v
            xc[0, row] = jnp.concatenate([zero_row, v[:-1]], axis=0)
            xc[2, row] = jnp.concatenate([v[1:], zero_row], axis=0)
            return 0
        lax.fori_loop(0, 4, body, 0)

    place(c)
    for d in range(1, nc):
        shares[d - 1].wait_recv()
        place(chan(nc - d))

    lane = lax.broadcasted_iota(jnp.int32, (64, 128), 1)
    group = 4

    def coarse(g, _):
        row = g * 4 * group
        lhs = jnp.concatenate(
            [
                xc[k, pl.ds(row + j, 4 * group)].reshape(128 * group, 256)
                for j in range(3) for k in range(3)
            ],
            axis=1,
        )
        got = jnp.dot(lhs, wcr[...], preferred_element_type=F32)
        for h in range(group):
            lo = got[h * 128 : h * 128 + 64]
            hi = got[h * 128 + 64 : h * 128 + 128]
            block = g * group + h
            con[0, block] = jnp.where(lane < 64, lo[:, :128], pltpu.roll(hi[:, :128], 64, 1)).astype(BF16)
            con[1, block] = jnp.where(lane < 64, pltpu.roll(lo[:, :128], 64, 1), hi[:, :128]).astype(BF16)
            con[2, block] = jnp.where(lane < 64, lo[:, 128:], pltpu.roll(hi[:, 128:], 64, 1)).astype(BF16)
        return 0
    lax.fori_loop(0, nc // group, coarse, 0)

    parts = []
    for i, brick in ((0, above), (1, b), (2, below)):
        for d in range(nc):
            if i == 1 and d == 0:
                continue
            copy = pltpu.make_async_remote_copy(
                con.at[i, chan(d)], rec.at[i, c], sc.at[i, d], rc.at[i, d],
                device_id=(brick, chan(d)), device_id_type=MESH,
            )
            copy.start()
            parts.append(copy)
    rec[1, c] = con[1, c]
    for part in parts:
        part.wait_recv()

    from_below, from_above = b > 0, b < nb - 1
    cols = []
    for k in range(nc):
        total = rec[1, k].astype(F32)
        total = total + jnp.where(from_below, rec[0, k].astype(F32), 0.0)
        total = total + jnp.where(from_above, rec[2, k].astype(F32), 0.0)
        cols.append(jnp.maximum(total, 0.0).astype(BF16))
    lifted = jnp.dot(jnp.concatenate(cols, axis=1), prr[...], preferred_element_type=F32)
    for r in range(4):
        for h in range(2):
            lanes = (r // 2) * 256 + h * 128
            piece = lifted[(r % 2) * 32 : (r % 2) * 32 + 32, lanes : lanes + 128]
            tmp[r, h, pl.ds(0, 32, stride=2)] = piece
            tmp[r, h, pl.ds(1, 32, stride=2)] = piece

    def merge(n, _):
        u = n // 8
        r = lax.rem(n, 8)
        plane = u + q * (1 - 2 * u)
        out[plane, r] = (
            skip[u, r].astype(F32) + jnp.concatenate([tmp[r // 2, 0], tmp[r // 2, 1]], axis=1)
        ).astype(BF16)
        return 0
    lax.fori_loop(0, 16, merge, 0)

    for copies in first + second:
        for copy in copies:
            copy.wait_send()
    for share in shares:
        share.wait_send()
    for part in parts:
        part.wait_send()


def shards(nb, nc, volume, first_weight, second_weight, coarse_weight, projection):
    dma = pltpu.SemaphoreType.DMA
    return pl.pallas_call(
        functools.partial(level, nb, nc),
        out_shape=jax.ShapeDtypeStruct(volume.shape, BF16),
        in_specs=[pl.BlockSpec(memory_space=pl.ANY)] * 5,
        out_specs=pl.BlockSpec(memory_space=pltpu.VMEM),
        scratch_shapes=[
            pltpu.VMEM((3, 4, 10, 64, 256), BF16),
            pltpu.VMEM((3, 4, 10, 64, 256), BF16),
            pltpu.VMEM((3, 2304, 256), BF16),
            pltpu.VMEM((3, 2304, 256), BF16),
            pltpu.VMEM((27, 256, 64), BF16),
            pltpu.VMEM((2304, 256), BF16),
            pltpu.VMEM((nc, 4, 32, 256), BF16),
            pltpu.VMEM((3, 4 * nc + 2, 32, 256), BF16),
            pltpu.VMEM((3, nc, 64, 128), BF16),
            pltpu.VMEM((3, nc, 64, 128), BF16),
            pltpu.VMEM((nc, 64, 256), BF16),
            pltpu.VMEM((nc * 128, 512), BF16),
            pltpu.VMEM((2, 512, 256), F32),
            pltpu.VMEM((2, 512, 256), F32),
            pltpu.VMEM((2, 8, 64, 256), BF16),
            pltpu.VMEM((4, 2, 64, 128), F32),
            dma((6,)),
            dma((2, 5)),
            dma((2, 5)),
            dma((2, 5)),
            dma((2, 5)),
            dma((nc,)),
            dma((nc,)),
            dma((nc,)),
            dma((nc,)),
            dma((3, nc)),
            dma((3, nc)),
        ],
        compiler_params=pltpu.CompilerParams(
            collective_id=0, has_side_effects=True, vmem_limit_bytes=56 << 20
        ),
        name="level",
    )(
        volume,
        first_weight.reshape(3, 2304, 256),
        second_weight.reshape(3, 2304, 256),
        coarse_weight.reshape(27, 256, 64),
        projection,
    )


def solution(mesh):
    in_specs = (
        P("brick", "chan", None, None),
        P(),
        P(),
        P(None, None, None, None, "chan"),
        P("chan", None),
    )
    out_specs = P("brick", "chan", None, None)
    body = functools.partial(shards, mesh.shape["brick"], mesh.shape["chan"])
    return jax.shard_map(body, mesh=mesh, in_specs=in_specs, out_specs=out_specs, check_vma=False)
```

time: 139 us -> 57.7 us (0.42)
  the two profiles are of different devices: /device:TPU:112 before, /device:TPU:1 now
where the time goes in v1:
time: 57.7 us; the launch traced here: 57.5 us
  Pallas kernels  53.1 us (92%)
  local copies, waits for them, and re-layouts  4.46 us (8%)
    pallas_call x1, Pallas kernels, shards(): pl.pallas_call(functools.partial(level, nb, nc), out_shape=jax.ShapeDtype...  53.1 us
    unnamed x2, local copies, waits for them, and re-layouts  4.46 us

profile of v1, /device:TPU:1, one launch (start us, length us, event | category | flops | bytes accessed | tf_op | source)
XLA Modules:
  0.0 57.5 jit_solution(2884385824434803841)
XLA Ops:
  0.0 2.6 %copy.6 = bf16[3,3,3,256,64]{4,3,2,1,0:T(8,128)(2,1)} copy(bf16[3,3,3,256,64]{3,4,2,1,0:T(8,128)(2,1)} %param.8) | data formatting | bytes 1769472 | tf_op args[3]
  2.6 53.1 %level.1 = bf16[2,8,64,256]{3,2,1,0:T(8,128)(2,1)} custom-call(bf16[2,8,64,256]{3,2,1,0:T(8,128)(2,1)} %vol.1, bf16[3,2304,256]{2,1,0:T(8,128)(2,1)} %bitcast.4, bf16[3,2304,256]{2,1,0:T(8,128)(2,1)} %bitcast.5, bf16[27,256,64]{2,1,0:T(8,128)(2,1)} %bitcast.3, bf16[64,256]{1,0:T(8,128)(2,1)} %prh.1), custom_call_target="tpu_custom_call" | custom-call | tf_op jit(solution)/shard_map/level/pallas_call | solution.py:313
  55.7 1.9 %copy.8 = bf16[2,8,64,256]{3,2,1,0:T(8,128)(2,1)} copy(bf16[2,8,64,256]{3,2,1,0:T(8,128)(2,1)} %level.1) | data formatting | bytes 1048576

commit v2 on v1

v2 whole, which is shorter than its diff:
```python
import functools

import jax
import jax.numpy as jnp
from jax import lax
from jax.experimental import pallas as pl
from jax.experimental.pallas import tpu as pltpu
from jax.sharding import PartitionSpec as P

MESH = pl.DeviceIdType.MESH
F32 = jnp.float32
BF16 = jnp.bfloat16


def level(
    nb, nc, vol, w1h, w2h, wch, prh, skip, lift,
    x, y, w1, w2, wc, xc, con, rec, prj, acc1, acc2, tmp,
    loc, s1, r1, s2, r2, sp, rp, sw, rw, sf, rf, sg, rg, sc, rc, near,
):
    b = lax.axis_index("brick")
    c = lax.axis_index("chan")
    q = lax.rem(b, 2)
    slow = lax.rem(b + 2 * q - 1 + nb, nb)
    fast = lax.rem(b + 1 - 2 * q + nb, nb)
    below = lax.rem(b - 1 + nb, nb)
    above = lax.rem(b + 1, nb)
    nx = nc // 2
    row_of, place = c // nx, lax.rem(c, nx)

    def chan(d):
        return lax.rem(c + d, nc)

    loads = [
        pltpu.make_async_copy(vol.at[q], x.at[1, 1, pl.ds(1, 8)], loc.at[0]),
        pltpu.make_async_copy(vol.at[1 - q], x.at[1, 2, pl.ds(1, 8)], loc.at[1]),
        pltpu.make_async_copy(w1h, w1, loc.at[2]),
        pltpu.make_async_copy(prh, prj.at[c], loc.at[3]),
        pltpu.make_async_copy(wch, wc.at[:, pl.ds(pl.multiple_of(place * 64, 64), 64)], loc.at[4]),
        pltpu.make_async_copy(w2h, w2, loc.at[5]),
    ]
    for k in (0, 1):
        loads[k].start()

    right, left, across = chan(1), chan(nc - 1), chan(nx)
    barrier = pltpu.get_barrier_semaphore()
    for who in ((slow, c), (b, right), (b, left), (b, across), (fast, right), (fast, left), (fast, c)):
        pl.semaphore_signal(barrier, inc=1, device_id=who, device_id_type=MESH)
    loads[0].wait()
    loads[1].wait()
    pl.semaphore_wait(barrier, 7)

    def halo(buf, ss, rs):
        plans = [(1, 1 + i, 1, 0, 1 + i, (slow, c)) for i in range(8)]
        plans += [
            (1, 1, 1, 1, 9, (b, left)),
            (1, 8, 1, 1, 0, (b, right)),
            (2, 1, 1, 2, 9, (b, left)),
            (2, 8, 1, 2, 0, (b, right)),
            (2, 1, 8, 3, 1, (fast, c)),
            (2, 1, 1, 3, 9, (fast, left)),
            (2, 8, 1, 3, 0, (fast, right)),
            (1, 1, 1, 0, 9, (slow, left)),
            (1, 8, 1, 0, 0, (slow, right)),
        ]
        return [
            pltpu.make_async_remote_copy(
                buf.at[1, src, pl.ds(row, n)], buf.at[1, dst, pl.ds(to, n)],
                ss.at[i], rs.at[i], device_id=who, device_id_type=MESH,
            )
            for i, (src, row, n, dst, to, who) in enumerate(plans)
        ]

    def start(copies, *which):
        for k in which:
            copies[k].start()

    def arrived(copies, *which):
        for k in which:
            copies[k].wait_recv()

    first = halo(x, s1, r1)
    start(first, 12, 8, 9, 10, 11, 0, 1, 2, 3, 4, 5, 6, 7, 13, 14)
    for who in (right, left, across):
        pl.semaphore_signal(near, inc=1, device_id=(b, who), device_id_type=MESH)
    for k in (2, 4, 3, 5):
        loads[k].start()

    gifts = [
        pltpu.make_async_remote_copy(
            prj.at[c], prj.at[c], sp.at[d], rp.at[d], device_id=(b, chan(d)), device_id_type=MESH
        )
        for d in range(1, nc)
    ]

    def shard(owner, core):
        return pl.ds(pl.multiple_of(owner * 64 + core * 32, 32), 32)

    def along(d):
        return lax.rem(place + d, nx)

    blocks = (pl.ds(0, 14), pl.ds(14, 13))

    def ring(slot, source, part, owner, to):
        return pltpu.make_async_remote_copy(
            source, wc.at[blocks[part], shard(owner, q)], sw.at[slot], rw.at[slot],
            device_id=(b, row_of * nx + to), device_id_type=MESH,
        )

    ahead, behind = along(1), along(nx - 1)
    mine = [wch.at[part, pl.ds(pl.multiple_of(q * 32, 32), 32)] for part in blocks]
    weights = [
        ring(0, mine[0], 0, place, ahead),
        ring(1, mine[1], 1, place, behind),
        ring(2, mine[1], 1, place, ahead),
        ring(3, mine[0], 0, place, behind),
        ring(4, wc.at[blocks[0], shard(behind, q)], 0, behind, ahead),
        ring(5, wc.at[blocks[1], shard(ahead, q)], 1, ahead, behind),
    ]
    passed = [
        pltpu.make_async_remote_copy(
            wc.at[:, shard(owner, q)], wc.at[:, shard(owner, q)], sf.at[d], rf.at[d],
            device_id=(fast, c), device_id_type=MESH,
        )
        for d, owner in enumerate((behind, ahead, along(nx // 2)))
    ]

    zero_row = jnp.zeros((1, 256), BF16)

    def spread(buf, p, row, v):
        buf[0, p, row] = jnp.concatenate([zero_row, v[:-1]], axis=0)
        buf[2, p, row] = jnp.concatenate([v[1:], zero_row], axis=0)

    def spread_rows(buf, p, start, n):
        def body(i, _):
            spread(buf, p, start + i, buf[1, p, start + i])
            return 0
        lax.fori_loop(0, n, body, 0)

    has_low, has_high = c > 0, c < nc - 1
    has_slow = jnp.logical_and(slow != b + nb - 1, slow != b + 1 - nb)

    def masked(buf, p, row, valid):
        v = jnp.where(valid, buf[1, p, row].astype(F32), 0.0).astype(BF16)
        buf[1, p, row] = v
        spread(buf, p, row, v)

    def edge_rows(buf, copies, u):
        arrived(copies, 8 + 2 * u, 9 + 2 * u)
        masked(buf, u + 1, 9, has_high)
        masked(buf, u + 1, 0, has_low)

    def slow_halo(buf, copies, part):
        if part == 0:
            arrived(copies, 0, 1, 2, 3, 4, 16)
            masked(buf, 0, 0, has_low)
            spread_rows(buf, 0, 1, 5)
        else:
            arrived(copies, 5, 6, 7, 15)
            masked(buf, 0, 9, has_high)
            spread_rows(buf, 0, 6, 3)

    def fast_halo(buf, copies):
        arrived(copies, 12, 13, 14)
        masked(buf, 3, 0, has_low)
        masked(buf, 3, 9, has_high)
        spread_rows(buf, 3, 1, 8)

    def taps(buf, w, u, i, row=0, n=8):
        lhs = jnp.concatenate(
            [
                buf[k, u + i, row + j : row + j + n].reshape(n * 64, 256)
                for j in range(3) for k in range(3)
            ],
            axis=1,
        )
        return jnp.dot(lhs, w[i + q * (2 - 2 * i)], preferred_element_type=F32)

    def slow_taps(buf, w, row, n):
        return jnp.where(has_slow, taps(buf, w, 0, 0, row, n), 0.0)

    def finish_one(u, start=0, n=8):
        def body(r, _):
            v = jnp.maximum(acc1[u, pl.ds(pl.multiple_of(r * 64, 64), 64)], 0.0).astype(BF16)
            y[1, u + 1, 1 + r] = v
            spread(y, u + 1, 1 + r, v)
            return 0
        lax.fori_loop(start, start + n, body, 0)

    pl.semaphore_wait(near, 3)
    start(first, 15, 16)
    start(weights, 0, 1, 2, 3)
    spread_rows(x, 1, 1, 8)
    spread_rows(x, 2, 1, 8)
    edge_rows(x, first, 0)
    edge_rows(x, first, 1)
    loads[2].wait()
    acc1[1] = taps(x, w1, 1, 0) + taps(x, w1, 1, 1)
    fast_halo(x, first)
    acc1[1] += taps(x, w1, 1, 2)
    finish_one(1)
    second = halo(y, s2, r2)
    start(second, 12, 10, 11, 13, 14)
    acc1[0] = taps(x, w1, 0, 1) + taps(x, w1, 0, 2)
    arrived(weights, 0, 1)
    start(weights, 4, 5)
    slow_halo(x, first, 0)
    acc1[0, :256] += slow_taps(x, w1, 0, 4)
    finish_one(0, 0, 4)
    start(second, 0, 15, 8, 1, 2, 3)
    slow_halo(x, first, 1)
    acc1[0, 256:] += slow_taps(x, w1, 4, 4)
    finish_one(0, 4, 4)
    start(second, 16, 9, 4, 5, 6, 7)

    loads[3].wait()
    for gift in gifts:
        gift.start()

    loads[5].wait()
    edge_rows(y, second, 1)
    acc2[1] = taps(y, w2, 1, 1)
    acc2[0] = taps(y, w2, 0, 2)
    fast_halo(y, second)
    acc2[1] += taps(y, w2, 1, 2)
    edge_rows(y, second, 0)
    acc2[1] += taps(y, w2, 1, 0)
    acc2[0] += taps(y, w2, 0, 1)
    loads[4].wait()
    arrived(weights, 2, 3)
    start(passed, 0, 1)
    slow_halo(y, second, 0)
    slow_halo(y, second, 1)
    acc2[0] += slow_taps(y, w2, 0, 8)
    def pool(r, _):
        total = jnp.zeros((64, 256), F32)
        for u in range(2):
            for s in range(2):
                rows = pl.ds(pl.multiple_of(r * 128 + s * 64, 64), 64)
                v = jnp.maximum(acc2[u, rows], 0.0).astype(BF16)
                skip[u + q * (1 - 2 * u), 2 * r + s] = v
                total = total + v.astype(F32)
        halves = []
        for h in range(2):
            tmp[r, h] = total[:, h * 128 : h * 128 + 128]
            even = tmp[r, h, pl.ds(0, 32, stride=2)]
            odd = tmp[r, h, pl.ds(1, 32, stride=2)]
            halves.append(((even + odd) * 0.125).astype(BF16))
        xc[1, row_of, 1 + r] = jnp.concatenate(halves, axis=1)
        return 0
    lax.fori_loop(0, 4, pool, 0)

    partner = across
    shares = [
        pltpu.make_async_remote_copy(
            xc.at[1, row_of, pl.ds(row, n)], xc.at[1, slot, pl.ds(to, n)],
            sg.at[i], rg.at[i], device_id=(b, who), device_id_type=MESH,
        )
        for i, (row, n, slot, to, who) in enumerate(
            [
                (1, 4, row_of, 1, partner),
                (4, 1, chan(1) // nx, 0, chan(1)),
                (4, 1, chan(1) // nx, 0, chan(1 + nx)),
                (1, 1, chan(nc - 1) // nx, 5, chan(nc - 1)),
                (1, 1, chan(nc - 1) // nx, 5, chan(nx - 1)),
            ]
        )
    ]
    for share in shares:
        share.start()
    arrived(weights, 4, 5)
    start(passed, 2)
    for share in shares:
        share.wait_recv()

    def widen(h, r, v):
        xc[0, h, r] = jnp.concatenate([zero_row, v[:-1]], axis=0)
        xc[2, h, r] = jnp.concatenate([v[1:], zero_row], axis=0)

    for h in range(2):
        block = h * nx + place
        for r, valid in ((0, block > 0), (5, block < nc - 1)):
            v = jnp.where(valid, xc[1, h, r].astype(F32), 0.0).astype(BF16)
            xc[1, h, r] = v
            widen(h, r, v)

        def coarse_row(r, _):
            widen(h, r, xc[1, h, r])
            return 0
        lax.fori_loop(1, 5, coarse_row, 0)
    arrived(passed, 0, 1, 2)

    parts = []
    for role, (tap, brick) in enumerate(((2 - 2 * q, slow), (1, b), (2 * q, fast))):
        lhs = jnp.concatenate(
            [xc[k, :, j : j + 4].reshape(256, 256) for j in range(3) for k in range(3)], axis=1
        )
        rhs = jnp.concatenate([wc[tap * 9 + jk] for jk in range(9)], axis=1)
        got = lax.dot_general(lhs, rhs, (((1,), (1,)), ((), ())), preferred_element_type=F32)
        con[role] = got.astype(BF16).reshape(2, 128, 256)
        for t, slot, who in ((0, row_of, c), (1, 1 - row_of, partner)):
            if role == 1 and t == 0:
                rec[1, row_of] = con[1, row_of]
                continue
            copy = pltpu.make_async_remote_copy(
                con.at[role, slot], rec.at[role, row_of], sc.at[role, t], rc.at[role, t],
                device_id=(brick, who), device_id_type=MESH,
            )
            copy.start()
            parts.append(copy)
    arrived(gifts, *range(nc - 1))
    for part in parts:
        part.wait_recv()

    cols = []
    for h in range(2):
        total = rec[1, h].astype(F32) + rec[2, h].astype(F32)
        total = total + jnp.where(has_slow, rec[0, h].astype(F32), 0.0)
        cols.append(jnp.maximum(total, 0.0).astype(BF16))
    lifted = jnp.dot(
        jnp.concatenate(cols, axis=1), prj[...].reshape(nc * 64, 256), preferred_element_type=F32
    )
    lift[...] = lifted.reshape(4, 32, 256)

    for copy in first + second + gifts + shares + parts + weights + passed:
        copy.wait_send()


def merge(skip, lift, out, tmp):
    for r in range(4):
        for h in range(2):
            piece = lift[r, :, h * 128 : h * 128 + 128]
            tmp[h, pl.ds(0, 32, stride=2)] = piece
            tmp[h, pl.ds(1, 32, stride=2)] = piece
        wide = jnp.concatenate([tmp[0], tmp[1]], axis=1)
        for u in range(2):
            for s in range(2):
                out[u, 2 * r + s] = (skip[u, 2 * r + s].astype(F32) + wide).astype(BF16)


def shards(nb, nc, volume, first_weight, second_weight, coarse_weight, projection):
    dma = pltpu.SemaphoreType.DMA
    skip, lift = pl.pallas_call(
        functools.partial(level, nb, nc),
        out_shape=(
            jax.ShapeDtypeStruct(volume.shape, BF16),
            jax.ShapeDtypeStruct((4, 32, 256), F32),
        ),
        in_specs=[pl.BlockSpec(memory_space=pl.ANY)] * 5,
        out_specs=(pl.BlockSpec(memory_space=pltpu.VMEM),) * 2,
        scratch_shapes=[
            pltpu.VMEM((3, 4, 10, 64, 256), BF16),
            pltpu.VMEM((3, 4, 10, 64, 256), BF16),
            pltpu.VMEM((3, 2304, 256), BF16),
            pltpu.VMEM((3, 2304, 256), BF16),
            pltpu.VMEM((27, 256, 256), BF16),
            pltpu.VMEM((3, 2, 6, 32, 256), BF16),
            pltpu.VMEM((3, 2, 128, 256), BF16),
            pltpu.VMEM((3, 2, 128, 256), BF16),
            pltpu.VMEM((nc, 64, 256), BF16),
            pltpu.VMEM((2, 512, 256), F32),
            pltpu.VMEM((2, 512, 256), F32),
            pltpu.VMEM((4, 2, 64, 128), F32),
            dma((6,)),
            dma((17,)),
            dma((17,)),
            dma((17,)),
            dma((17,)),
            dma((nc,)),
            dma((nc,)),
            dma((6,)),
            dma((6,)),
            dma((3,)),
            dma((3,)),
            dma((5,)),
            dma((5,)),
            dma((3, 2)),
            dma((3, 2)),
            pltpu.SemaphoreType.REGULAR,
        ],
        compiler_params=pltpu.CompilerParams(
            collective_id=0, has_side_effects=True, vmem_limit_bytes=56 << 20
        ),
        name="level",
    )(
        volume,
        first_weight.reshape(3, 2304, 256),
        second_weight.reshape(3, 2304, 256),
        jnp.swapaxes(coarse_weight, 3, 4).reshape(27, 64, 256),
        projection,
    )
    return pl.pallas_call(
        merge,
        out_shape=jax.ShapeDtypeStruct(volume.shape, BF16),
        scratch_shapes=[pltpu.VMEM((2, 64, 128), F32)],
        name="merge",
    )(skip, lift)


def solution(mesh):
    in_specs = (
        P("brick", "chan", None, None),
        P(),
        P(),
        P(None, None, None, None, "chan"),
        P("chan", None),
    )
    out_specs = P("brick", "chan", None, None)
    body = functools.partial(shards, mesh.shape["brick"], mesh.shape["chan"])
    return jax.shard_map(body, mesh=mesh, in_specs=in_specs, out_specs=out_specs, check_vma=False)
```

time: 57.7 us -> 48.5 us (0.84)
  Pallas kernels: 53.1 us -> 48.4 us
  local copies, waits for them, and re-layouts: 4.46 us -> 0 us
    pallas_call x1 -> x2, Pallas kernels: 53.1 us -> 48.4 us  [the longest x1 46.5 us: shards(): pl.pallas_call(functools.partial(level, nb, nc), out_shape=(jax.ShapeDtyp...]
    unnamed x2 -> x0, local copies, waits for them, and re-layouts: 4.46 us -> none
where the time goes in v2:
time: 48.5 us; the launch traced here: 48.4 us
  Pallas kernels  48.4 us (100%)
    pallas_call x1, Pallas kernels, shards(): pl.pallas_call(functools.partial(level, nb, nc), out_shape=(jax.ShapeDtyp...  46.5 us
    pallas_call x1, Pallas kernels, shards(): pl.pallas_call(merge, out_shape=jax.ShapeDtypeStruct(volume.shape, BF16),...  1.95 us

profile of v2, /device:TPU:1, one launch (start us, length us, event | category | flops | bytes accessed | tf_op | source)
XLA Modules:
  0.0 48.4 jit_solution(13278275506765586713)
XLA Ops:
  0.0 46.5 %level.1 = (bf16[2,8,64,256]{3,2,1,0:T(8,128)(2,1)}, f32[4,32,256]{2,1,0:T(8,128)}) custom-call(bf16[2,8,64,256]{3,2,1,0:T(8,128)(2,1)} %vol.1, bf16[3,2304,256]{2,1,0:T(8,128)(2,1)} %bitcast.5, bf16[3,2304,256]{2,1,0:T(8,128)(2,1)} %bitcast.6, bf16[27,64,256]{2,1,0:T(8,128)(2,1)} %bitcast.7, bf16[64,256]{1,0:T(8,128)(2,1)} %prh.1), custom_call_target="tpu_custom_call" | custom-call | tf_op jit(solution)/shard_map/level/pallas_call | solution.py:342
  46.5 2.0 %merge.1 = bf16[2,8,64,256]{3,2,1,0:T(8,128)(2,1)} custom-call(bf16[2,8,64,256]{3,2,1,0:T(8,128)(2,1)} %get-tuple-element.7.skip, f32[4,32,256]{2,1,0:T(8,128)} %get-tuple-element.8.lift), custom_call_target="tpu_custom_call" | custom-call | tf_op jit(solution)/shard_map/merge/pallas_call | solution.py:391

commit v3 on v2

--- a/solution.py
+++ b/solution.py
@@ -82,14 +82,17 @@
     start(first, 12, 8, 9, 10, 11, 0, 1, 2, 3, 4, 5, 6, 7, 13, 14)
     for who in (right, left, across):
         pl.semaphore_signal(near, inc=1, device_id=(b, who), device_id_type=MESH)
-    for k in (2, 4, 3, 5):
+    for k in (3, 2, 4, 5):
         loads[k].start()
 
     gifts = [
         pltpu.make_async_remote_copy(
-            prj.at[c], prj.at[c], sp.at[d], rp.at[d], device_id=(b, chan(d)), device_id_type=MESH
-        )
-        for d in range(1, nc)
+            prj.at[block], prj.at[block], sp.at[i], rp.at[i],
+            device_id=(b, row_of * nx + lax.rem(place + d, nx) if d else across), device_id_type=MESH,
+        )
+        for i, (block, d) in enumerate(
+            [(c, 0)] + [(block, d) for d in range(1, nx) for block in (c, across)]
+        )
     ]
 
     def shard(owner, core):
@@ -134,7 +137,7 @@
         def body(i, _):
             spread(buf, p, start + i, buf[1, p, start + i])
             return 0
-        lax.fori_loop(0, n, body, 0)
+        lax.fori_loop(0, n, body, 0, unroll=4)
 
     has_low, has_high = c > 0, c < nc - 1
     has_slow = jnp.logical_and(slow != b + nb - 1, slow != b + 1 - nb)
@@ -149,15 +152,14 @@
         masked(buf, u + 1, 9, has_high)
         masked(buf, u + 1, 0, has_low)
 
-    def slow_halo(buf, copies, part):
-        if part == 0:
-            arrived(copies, 0, 1, 2, 3, 4, 16)
-            masked(buf, 0, 0, has_low)
-            spread_rows(buf, 0, 1, 5)
-        else:
-            arrived(copies, 5, 6, 7, 15)
-            masked(buf, 0, 9, has_high)
-            spread_rows(buf, 0, 6, 3)
+    def slow_rows(buf, copies):
+        arrived(copies, *range(8))
+        spread_rows(buf, 0, 1, 8)
+
+    def slow_corners(buf, copies):
+        arrived(copies, 15, 16)
+        masked(buf, 0, 0, has_low)
+        masked(buf, 0, 9, has_high)
 
     def fast_halo(buf, copies):
         arrived(copies, 12, 13, 14)
@@ -175,8 +177,20 @@
         )
         return jnp.dot(lhs, w[i + q * (2 - 2 * i)], preferred_element_type=F32)
 
-    def slow_taps(buf, w, row, n):
-        return jnp.where(has_slow, taps(buf, w, 0, 0, row, n), 0.0)
+    def slow_middle(acc, buf, w):
+        acc[0, 64:448] += jnp.where(has_slow, taps(buf, w, 0, 0, 1, 6), 0.0)
+
+    def slow_edges(acc, buf, w):
+        lhs = jnp.concatenate(
+            [
+                jnp.concatenate([buf[k, 0, j], buf[k, 0, 7 + j]], axis=0)
+                for j in range(3) for k in range(3)
+            ],
+            axis=1,
+        )
+        got = jnp.where(has_slow, jnp.dot(lhs, w[2 * q], preferred_element_type=F32), 0.0)
+        acc[0, 0:64] += got[:64]
+        acc[0, 448:512] += got[64:]
 
     def finish_one(u, start=0, n=8):
         def body(r, _):
@@ -189,6 +203,8 @@
     pl.semaphore_wait(near, 3)
     start(first, 15, 16)
     start(weights, 0, 1, 2, 3)
+    loads[3].wait()
+    start(gifts, 0)
     spread_rows(x, 1, 1, 8)
     spread_rows(x, 2, 1, 8)
     edge_rows(x, first, 0)
@@ -203,18 +219,15 @@
     acc1[0] = taps(x, w1, 0, 1) + taps(x, w1, 0, 2)
     arrived(weights, 0, 1)
     start(weights, 4, 5)
-    slow_halo(x, first, 0)
-    acc1[0, :256] += slow_taps(x, w1, 0, 4)
-    finish_one(0, 0, 4)
-    start(second, 0, 15, 8, 1, 2, 3)
-    slow_halo(x, first, 1)
-    acc1[0, 256:] += slow_taps(x, w1, 4, 4)
-    finish_one(0, 4, 4)
-    start(second, 16, 9, 4, 5, 6, 7)
-
-    loads[3].wait()
-    for gift in gifts:
-        gift.start()
+    slow_rows(x, first)
+    slow_middle(acc1, x, w1)
+    finish_one(0, 1, 6)
+    start(second, 1, 2, 3, 4, 5, 6)
+    slow_corners(x, first)
+    slow_edges(acc1, x, w1)
+    finish_one(0, 0, 1)
+    finish_one(0, 7, 1)
+    start(second, 15, 16, 0, 7, 8, 9)
 
     loads[5].wait()
     edge_rows(y, second, 1)
@@ -228,9 +241,10 @@
     loads[4].wait()
     arrived(weights, 2, 3)
     start(passed, 0, 1)
-    slow_halo(y, second, 0)
-    slow_halo(y, second, 1)
-    acc2[0] += slow_taps(y, w2, 0, 8)
+    slow_rows(y, second)
+    slow_middle(acc2, y, w2)
+    slow_corners(y, second)
+    slow_edges(acc2, y, w2)
     def pool(r, _):
         total = jnp.zeros((64, 256), F32)
         for u in range(2):
@@ -247,7 +261,7 @@
             halves.append(((even + odd) * 0.125).astype(BF16))
         xc[1, row_of, 1 + r] = jnp.concatenate(halves, axis=1)
         return 0
-    lax.fori_loop(0, 4, pool, 0)
+    lax.fori_loop(0, 4, pool, 0, unroll=2)
 
     partner = across
     shares = [
@@ -267,6 +281,8 @@
     ]
     for share in shares:
         share.start()
+    arrived(gifts, 0)
+    start(gifts, *range(1, 2 * nx - 1))
     arrived(weights, 4, 5)
     start(passed, 2)
     for share in shares:
@@ -286,7 +302,7 @@
         def coarse_row(r, _):
             widen(h, r, xc[1, h, r])
             return 0
-        lax.fori_loop(1, 5, coarse_row, 0)
+        lax.fori_loop(1, 5, coarse_row, 0, unroll=4)
     arrived(passed, 0, 1, 2)
 
     parts = []
@@ -307,7 +323,7 @@
             )
             copy.start()
             parts.append(copy)
-    arrived(gifts, *range(nc - 1))
+    arrived(gifts, *range(1, 2 * nx - 1))
     for part in parts:
         part.wait_recv()
 
@@ -325,16 +341,32 @@
         copy.wait_send()
 
 
-def merge(skip, lift, out, tmp):
+def merge(skip, lift, out, cells, done, rows, tmp, come, go):
+    whole = pltpu.make_async_copy(lift, rows, come.at[8])
+    whole.start()
+    loads = [
+        pltpu.make_async_copy(skip.at[u, pl.ds(2 * r, 2)], cells.at[u, r], come.at[2 * r + u])
+        for r in range(4) for u in range(2)
+    ]
+    for load in loads:
+        load.start()
+    whole.wait()
+    stores = []
     for r in range(4):
         for h in range(2):
-            piece = lift[r, :, h * 128 : h * 128 + 128]
-            tmp[h, pl.ds(0, 32, stride=2)] = piece
-            tmp[h, pl.ds(1, 32, stride=2)] = piece
-        wide = jnp.concatenate([tmp[0], tmp[1]], axis=1)
+            piece = rows[r, :, h * 128 : h * 128 + 128]
+            tmp[r, h, pl.ds(0, 32, stride=2)] = piece
+            tmp[r, h, pl.ds(1, 32, stride=2)] = piece
+        wide = jnp.concatenate([tmp[r, 0], tmp[r, 1]], axis=1)
         for u in range(2):
+            loads[2 * r + u].wait()
             for s in range(2):
-                out[u, 2 * r + s] = (skip[u, 2 * r + s].astype(F32) + wide).astype(BF16)
+                done[u, r, s] = (cells[u, r, s].astype(F32) + wide).astype(BF16)
+            store = pltpu.make_async_copy(done.at[u, r], out.at[u, pl.ds(2 * r, 2)], go.at[2 * r + u])
+            store.start()
+            stores.append(store)
+    for store in stores:
+        store.wait()
 
 
 def shards(nb, nc, volume, first_weight, second_weight, coarse_weight, projection):
@@ -391,7 +423,17 @@
     return pl.pallas_call(
         merge,
         out_shape=jax.ShapeDtypeStruct(volume.shape, BF16),
-        scratch_shapes=[pltpu.VMEM((2, 64, 128), F32)],
+        in_specs=[pl.BlockSpec(memory_space=pl.ANY)] * 2,
+        out_specs=pl.BlockSpec(memory_space=pl.ANY),
+        scratch_shapes=[
+            pltpu.VMEM((2, 4, 2, 64, 256), BF16),
+            pltpu.VMEM((2, 4, 2, 64, 256), BF16),
+            pltpu.VMEM((4, 32, 256), F32),
+            pltpu.VMEM((4, 2, 64, 128), F32),
+            dma((9,)),
+            dma((8,)),
+        ],
+        compiler_params=pltpu.CompilerParams(vmem_limit_bytes=63 << 20),
         name="merge",
     )(skip, lift)
 

time: 48.5 us -> 46.8 us (0.965)
  Pallas kernels: 48.4 us -> 46.7 us
    pallas_call x1, Pallas kernels: 46.5 us -> 44.8 us  [shards(): pl.pallas_call(functools.partial(level, nb, nc), out_shape=(jax.ShapeDtyp...]
where the time goes in v3:
time: 46.8 us; the launch traced here: 46.7 us
  Pallas kernels  46.7 us (100%)
    pallas_call x1, Pallas kernels, shards(): pl.pallas_call(functools.partial(level, nb, nc), out_shape=(jax.ShapeDtyp...  44.8 us
    pallas_call x1, Pallas kernels, shards(): pl.pallas_call(merge, out_shape=jax.ShapeDtypeStruct(volume.shape, BF16),...  1.9 us

profile of v3, /device:TPU:1, one launch (start us, length us, event | category | flops | bytes accessed | tf_op | source)
XLA Modules:
  0.0 46.7 jit_solution(15156776194488324096)
XLA Ops:
  0.0 44.8 %level.1 = (bf16[2,8,64,256]{3,2,1,0:T(8,128)(2,1)}, f32[4,32,256]{2,1,0:T(8,128)}) custom-call(bf16[2,8,64,256]{3,2,1,0:T(8,128)(2,1)} %vol.1, bf16[3,2304,256]{2,1,0:T(8,128)(2,1)} %bitcast.5, bf16[3,2304,256]{2,1,0:T(8,128)(2,1)} %bitcast.6, bf16[27,64,256]{2,1,0:T(8,128)(2,1)} %bitcast.7, bf16[64,256]{1,0:T(8,128)(2,1)} %prh.1), custom_call_target="tpu_custom_call" | custom-call | tf_op jit(solution)/shard_map/level/pallas_call | solution.py:374
  44.8 1.9 %merge.1 = bf16[2,8,64,256]{3,2,1,0:T(8,128)(2,1)} custom-call(bf16[2,8,64,256]{3,2,1,0:T(8,128)(2,1)} %get-tuple-element.7.skip, f32[4,32,256]{2,1,0:T(8,128)} %get-tuple-element.8.lift), custom_call_target="tpu_custom_call" | custom-call | tf_op jit(solution)/shard_map/merge/pallas_call | solution.py:423

commit v4 on v3

--- a/solution.py
+++ b/solution.py
@@ -410,15 +410,20 @@
             pltpu.SemaphoreType.REGULAR,
         ],
         compiler_params=pltpu.CompilerParams(
-            collective_id=0, has_side_effects=True, vmem_limit_bytes=56 << 20
+            collective_id=0, has_side_effects=True, vmem_limit_bytes=50 << 20
         ),
         name="level",
     )(
-        volume,
-        first_weight.reshape(3, 2304, 256),
-        second_weight.reshape(3, 2304, 256),
-        jnp.swapaxes(coarse_weight, 3, 4).reshape(27, 64, 256),
-        projection,
+        *(
+            pltpu.with_memory_space_constraint(v, pltpu.HBM)
+            for v in (
+                volume,
+                first_weight.reshape(3, 2304, 256),
+                second_weight.reshape(3, 2304, 256),
+                jnp.swapaxes(coarse_weight, 3, 4).reshape(27, 64, 256),
+                projection,
+            )
+        )
     )
     return pl.pallas_call(
         merge,
@@ -433,7 +438,7 @@
             dma((9,)),
             dma((8,)),
         ],
-        compiler_params=pltpu.CompilerParams(vmem_limit_bytes=63 << 20),
+        compiler_params=pltpu.CompilerParams(vmem_limit_bytes=8 << 20),
         name="merge",
     )(skip, lift)
 

time: 46.8 us -> 45.8 us (0.979)
  Pallas kernels: 46.7 us -> 45.7 us
    pallas_call x1, Pallas kernels: 44.8 us -> 43.9 us  [shards(): pl.pallas_call(functools.partial(level, nb, nc), out_shape=(jax.ShapeDtyp...]
where the time goes in v4:
time: 45.8 us
  Pallas kernels  45.7 us (100%)
    pallas_call x1, Pallas kernels, shards(): pl.pallas_call(functools.partial(level, nb, nc), out_shape=(jax.ShapeDtyp...  43.9 us
    pallas_call x1, Pallas kernels, shards(): pl.pallas_call(merge, out_shape=jax.ShapeDtypeStruct(volume.shape, BF16),...  1.8 us

profile of v4, /device:TPU:1, one launch (start us, length us, event | category | flops | bytes accessed | tf_op | source)
XLA Modules:
  0.0 45.8 jit_solution(5195561876766239519)
XLA Ops:
  0.0 43.9 %level.1 = (bf16[2,8,64,256]{3,2,1,0:T(8,128)(2,1)S(1)}, f32[4,32,256]{2,1,0:T(8,128)S(1)}) custom-call(bf16[2,8,64,256]{3,2,1,0:T(8,128)(2,1)} %vol.1, bf16[3,2304,256]{2,1,0:T(8,128)(2,1)} %bitcast.5, bf16[3,2304,256]{2,1,0:T(8,128)(2,1)} %bitcast.6, bf16[27,64,256]{2,1,0:T(8,128)(2,1)} %bitcast.7, bf16[64,256]{1,0:T(8,128)(2,1)} %prh.1), custom_call_target="tpu_custom_call" | custom-call | tf_op jit(solution)/shard_map/level/pallas_call | solution.py:374
  44.0 1.8 %merge.1 = bf16[2,8,64,256]{3,2,1,0:T(8,128)(2,1)} custom-call(bf16[2,8,64,256]{3,2,1,0:T(8,128)(2,1)S(1)} %get-tuple-element.7.skip, f32[4,32,256]{2,1,0:T(8,128)S(1)} %get-tuple-element.8.lift), custom_call_target="tpu_custom_call" | custom-call | tf_op jit(solution)/shard_map/merge/pallas_call | solution.py:428

commit v5 on v4

--- a/solution.py
+++ b/solution.py
@@ -306,32 +306,42 @@
     arrived(passed, 0, 1, 2)
 
     parts = []
-    for role, (tap, brick) in enumerate(((2 - 2 * q, slow), (1, b), (2 * q, fast))):
+    for role, tap, brick in ((0, 2 - 2 * q, slow), (2, 2 * q, fast), (1, 1, b)):
         lhs = jnp.concatenate(
             [xc[k, :, j : j + 4].reshape(256, 256) for j in range(3) for k in range(3)], axis=1
         )
         rhs = jnp.concatenate([wc[tap * 9 + jk] for jk in range(9)], axis=1)
         got = lax.dot_general(lhs, rhs, (((1,), (1,)), ((), ())), preferred_element_type=F32)
         con[role] = got.astype(BF16).reshape(2, 128, 256)
+        if role == 1:
+            parts[3].wait_recv()
+            joint = con[1, 1 - row_of].astype(F32) + rec[2, 1 - row_of].astype(F32)
+            con[1, 1 - row_of] = joint.astype(BF16)
         for t, slot, who in ((0, row_of, c), (1, 1 - row_of, partner)):
             if role == 1 and t == 0:
                 rec[1, row_of] = con[1, row_of]
                 continue
             copy = pltpu.make_async_remote_copy(
-                con.at[role, slot], rec.at[role, row_of], sc.at[role, t], rc.at[role, t],
-                device_id=(brick, who), device_id_type=MESH,
+                con.at[role, slot],
+                rec.at[role, slot if role == 2 else row_of],
+                sc.at[role, t], rc.at[role, t],
+                device_id=(brick, c if role == 2 else who), device_id_type=MESH,
             )
             copy.start()
             parts.append(copy)
     arrived(gifts, *range(1, 2 * nx - 1))
-    for part in parts:
+    for part in parts[:3] + parts[4:]:
         part.wait_recv()
 
-    cols = []
-    for h in range(2):
-        total = rec[1, h].astype(F32) + rec[2, h].astype(F32)
-        total = total + jnp.where(has_slow, rec[0, h].astype(F32), 0.0)
-        cols.append(jnp.maximum(total, 0.0).astype(BF16))
+    own = rec[1, row_of].astype(F32) + rec[2, row_of].astype(F32)
+    own = own + jnp.where(has_slow, rec[0, row_of].astype(F32), 0.0)
+    other = rec[1, 1 - row_of].astype(F32)
+    other = other + jnp.where(has_slow, rec[0, 1 - row_of].astype(F32), 0.0)
+    own, other = jnp.maximum(own, 0.0), jnp.maximum(other, 0.0)
+    cols = [
+        jnp.where(row_of == 0, own, other).astype(BF16),
+        jnp.where(row_of == 0, other, own).astype(BF16),
+    ]
     lifted = jnp.dot(
         jnp.concatenate(cols, axis=1), prj[...].reshape(nc * 64, 256), preferred_element_type=F32
     )

time: 45.8 us -> 46.3 us (1.011)
  Pallas kernels: 45.7 us -> 46.2 us
    pallas_call x1, Pallas kernels: 43.9 us -> 44.4 us  [shards(): pl.pallas_call(functools.partial(level, nb, nc), out_shape=(jax.ShapeDtyp...]
where the time goes in v5:
time: 46.3 us; the launch traced here: 46.2 us
  Pallas kernels  46.2 us (100%)
    pallas_call x1, Pallas kernels, shards(): pl.pallas_call(functools.partial(level, nb, nc), out_shape=(jax.ShapeDtyp...  44.4 us
    pallas_call x1, Pallas kernels, shards(): pl.pallas_call(merge, out_shape=jax.ShapeDtypeStruct(volume.shape, BF16),...  1.8 us

profile of v5, /device:TPU:1, one launch (start us, length us, event | category | flops | bytes accessed | tf_op | source)
XLA Modules:
  0.0 46.2 jit_solution(18197536466574662677)
XLA Ops:
  0.0 44.4 %level.1 = (bf16[2,8,64,256]{3,2,1,0:T(8,128)(2,1)S(1)}, f32[4,32,256]{2,1,0:T(8,128)S(1)}) custom-call(bf16[2,8,64,256]{3,2,1,0:T(8,128)(2,1)} %vol.1, bf16[3,2304,256]{2,1,0:T(8,128)(2,1)} %bitcast.5, bf16[3,2304,256]{2,1,0:T(8,128)(2,1)} %bitcast.6, bf16[27,64,256]{2,1,0:T(8,128)(2,1)} %bitcast.7, bf16[64,256]{1,0:T(8,128)(2,1)} %prh.1), custom_call_target="tpu_custom_call" | custom-call | tf_op jit(solution)/shard_map/level/pallas_call | solution.py:384
  44.4 1.8 %merge.1 = bf16[2,8,64,256]{3,2,1,0:T(8,128)(2,1)} custom-call(bf16[2,8,64,256]{3,2,1,0:T(8,128)(2,1)S(1)} %get-tuple-element.7.skip, f32[4,32,256]{2,1,0:T(8,128)S(1)} %get-tuple-element.8.lift), custom_call_target="tpu_custom_call" | custom-call | tf_op jit(solution)/shard_map/merge/pallas_call | solution.py:438
